TPU v7x, 128 devices: a whole 4x4x4 slice. The times are simulated.
128 devices in a mesh: section: 2 (over core), dp: 64 (over y, z, x).
Axes of the slice: x: 4, y: 4, z: 4, core: 2. Of those that a mesh axis runs over, the one named last changes fastest.
Arguments:
- inputs: bfloat16 [2, 4096, 960], P(None, 'dp'), may hold values from -16 to 16
- starts: int32 [2, 4096], P(None, 'dp'), may hold values from 0 to 64, as said below
- cotangent: bfloat16 [2, 4096, 960], P(None, 'dp'), may hold values from -16 to 16
- w_query: bfloat16 [2, 960, 960], P('section', 'dp'), may hold values from -0.1875 to 0.1875
- w_key: bfloat16 [2, 960, 320], P('section', 'dp'), may hold values from -0.1875 to 0.1875
- w_value: bfloat16 [2, 960, 320], P('section', 'dp'), may hold values from -0.1875 to 0.1875
- w_output: bfloat16 [2, 960, 960], P('section', 'dp'), may hold values from -0.75 to 0.75
- w_gate: bfloat16 [2, 960, 2560], P('section', 'dp'), may hold values from -0.1875 to 0.1875
- w_up: bfloat16 [2, 960, 2560], P('section', 'dp'), may hold values from -0.1875 to 0.1875
- w_down: bfloat16 [2, 2560, 960], P('section', 'dp'), may hold values from -0.15625 to 0.15625
- attn_gain: bfloat16 [2, 960], P('section', 'dp'), may hold values from 0.25 to 1.75
- ffn_gain: bfloat16 [2, 960], P('section', 'dp'), may hold values from 0.25 to 1.75
Outputs:
- activations: bfloat16 [2, 2, 4096, 960], P('section', None, 'dp')
- input_grads: bfloat16 [2, 2, 4096, 960], P('section', None, 'dp')
- grad_query: float32 [2, 960, 960], P('section', 'dp')
- grad_key: float32 [2, 960, 320], P('section', 'dp')
- grad_value: float32 [2, 960, 320], P('section', 'dp')
- grad_output: float32 [2, 960, 960], P('section', 'dp')
- grad_gate: float32 [2, 960, 2560], P('section', 'dp')
- grad_up: float32 [2, 960, 2560], P('section', 'dp')
- grad_down: float32 [2, 2560, 960], P('section', 'dp')
- grad_attn_gain: float32 [2, 960], P('section', 'dp')
- grad_ffn_gain: float32 [2, 960], P('section', 'dp')
Inputs may be any that keep to these rules, and one draw needn't show every extreme that they name: `starts`: within each aligned block of 64 rows (one index of dp, one micro-batch) sequences lie end to end from the block's first row, each row holding the block-local index of its sequence's first row; the rows after the last sequence are padding and hold 64. At least a quarter of every block's rows are in sequences, and some blocks are full.
All inputs are finite; a program needn't handle non-finite values.
Results may differ from a plain program's by a relative error of at most 0.023.
Values may be sent and summed in bfloat16 or wider, within the bound.
No kernel may reach another device: no remote copies, remote signals or barrier semaphores. Data moves between devices by JAX's collectives and lax.ppermute only.
A program may use at most 256 MiB of HBM per device.

v0:
```python
from functools import partial
import jax
import jax.numpy as jnp
from jax import lax
from jax.sharding import PartitionSpec as P

D = 960
HEADS = 15
KV_HEADS = 5
HEAD_DIM = 64
FF = 2560
QD = 960
KVD = 320
norm_eps = 1e-05
masked_score = -1e30
rope_base = 10000.0


def from_behind(value, axis, steps):
    count = lax.axis_size(axis)
    first, last = (max(0, -steps), min(count, count - steps))
    return lax.ppermute(value, axis, [(source, source + steps) for source in range(first, last)])


def rms_scale(values, gain):
    inverse = lax.rsqrt(jnp.mean(values * values, axis=-1, keepdims=True) + norm_eps)
    return values * inverse * gain


def rotate(values, cosine_table, sine_table):
    half_dim = values.shape[-1] // 2
    first_half = values[..., :half_dim]
    second_half = values[..., half_dim:]
    return jnp.concatenate(
        [
            first_half * cosine_table - second_half * sine_table,
            second_half * cosine_table + first_half * sine_table,
        ],
        axis=-1,
    )


def swiglu(gate_vals, up_vals):
    return jax.nn.silu(gate_vals) * up_vals


def right_trans(left, matrix):
    return lax.dot_general(
        left, matrix, (((1,), (1,)), ((), ())), preferred_element_type=jnp.float32
    )


def cross_rows(left, right):
    left_flat = left.reshape(-1, left.shape[-1])
    right_flat = right.reshape(-1, right.shape[-1])
    return lax.dot_general(
        left_flat, right_flat, (((0,), (0,)), ((), ())), preferred_element_type=jnp.float32
    )


def geometry(starts):
    row_count = starts.shape[0]
    local_rows = jnp.arange(row_count, dtype=jnp.int32)
    live_mask = starts <= local_rows
    position = jnp.where(live_mask, local_rows - starts, 0).astype(jnp.float32)
    frequency = rope_base ** (-2.0 * jnp.arange(HEAD_DIM // 2, dtype=jnp.float32) / HEAD_DIM)
    angles = position[:, None, None] * frequency[None, None, :]
    causal = local_rows[None, :] <= local_rows[:, None]
    inside = local_rows[None, :] >= starts[:, None]
    diagonal = local_rows[None, :] == local_rows[:, None]
    allowed = causal & inside | diagonal
    return (live_mask.astype(jnp.float32)[:, None], jnp.cos(angles), jnp.sin(angles), allowed)


def attention_block(normed_low, weights, cosine_table, sine_table, allowed):
    w_query, w_key, w_value = (weights[0], weights[1], weights[2])
    row_count = normed_low.shape[0]
    group_size = HEADS // KV_HEADS
    query_raw = jnp.dot(normed_low, w_query, preferred_element_type=jnp.float32)
    key_raw = jnp.dot(normed_low, w_key, preferred_element_type=jnp.float32)
    value_raw = jnp.dot(normed_low, w_value, preferred_element_type=jnp.float32)
    query_rot = rotate(
        query_raw.reshape(row_count, HEADS, HEAD_DIM), cosine_table, sine_table
    ).astype(jnp.bfloat16)
    key_rot = rotate(
        key_raw.reshape(row_count, KV_HEADS, HEAD_DIM), cosine_table, sine_table
    ).astype(jnp.bfloat16)
    value_heads = value_raw.astype(jnp.bfloat16).reshape(row_count, KV_HEADS, HEAD_DIM)
    grouped = query_rot.reshape(row_count, KV_HEADS, group_size, HEAD_DIM)
    scores = jnp.einsum(
        "qhgd,khd->hgqk", grouped, key_rot, preferred_element_type=jnp.float32
    ) * HEAD_DIM ** (-0.5)
    scores = jnp.where(allowed[None, None], scores, masked_score)
    row_peak = jnp.max(scores, axis=-1, keepdims=True)
    exp_scores = jnp.exp(scores - row_peak)
    probs_f32 = exp_scores / jnp.sum(exp_scores, axis=-1, keepdims=True)
    probs_low = probs_f32.astype(jnp.bfloat16)
    mixed_f32 = jnp.einsum(
        "hgqk,khd->qhgd", probs_low, value_heads, preferred_element_type=jnp.float32
    )
    mixed_low = mixed_f32.reshape(row_count, HEADS * HEAD_DIM).astype(jnp.bfloat16)
    return (mixed_low, (grouped, key_rot, value_heads, probs_f32, probs_low))


def layer_forward(source, weights, starts):
    w_query, w_key, w_value, w_output, w_gate, w_up, w_down, attn_gain, ffn_gain = weights
    live_rows, cosine_table, sine_table, allowed = geometry(starts)
    rows_f32 = source.astype(jnp.float32)
    normed_low = rms_scale(rows_f32, attn_gain.astype(jnp.float32)).astype(jnp.bfloat16)
    mixed_low, unused_saved = attention_block(
        normed_low, weights, cosine_table, sine_table, allowed
    )
    middle = rows_f32 + jnp.dot(mixed_low, w_output, preferred_element_type=jnp.float32)
    second_low = rms_scale(middle, ffn_gain.astype(jnp.float32)).astype(jnp.bfloat16)
    gate_vals = jnp.dot(second_low, w_gate, preferred_element_type=jnp.float32)
    up_vals = jnp.dot(second_low, w_up, preferred_element_type=jnp.float32)
    hidden_low = swiglu(gate_vals, up_vals).astype(jnp.bfloat16)
    result = (middle + jnp.dot(hidden_low, w_down, preferred_element_type=jnp.float32)) * live_rows
    return result.astype(jnp.bfloat16)


def layer_backward(source, weights, starts, upstream):
    w_query, w_key, w_value, w_output, w_gate, w_up, w_down, attn_gain, ffn_gain = weights
    live_rows, cosine_table, sine_table, allowed = geometry(starts)
    row_count = source.shape[0]
    group_size = HEADS // KV_HEADS
    score_scale = HEAD_DIM ** (-0.5)
    rows_f32 = source.astype(jnp.float32)
    first_normed, first_back = jax.vjp(rms_scale, rows_f32, attn_gain.astype(jnp.float32))
    normed_low = first_normed.astype(jnp.bfloat16)
    mixed_low, saved = attention_block(normed_low, weights, cosine_table, sine_table, allowed)
    grouped, key_rot, value_heads, probs_f32, probs_low = saved
    middle = rows_f32 + jnp.dot(mixed_low, w_output, preferred_element_type=jnp.float32)
    second_normed, second_back = jax.vjp(rms_scale, middle, ffn_gain.astype(jnp.float32))
    second_low = second_normed.astype(jnp.bfloat16)
    gate_vals = jnp.dot(second_low, w_gate, preferred_element_type=jnp.float32)
    up_vals = jnp.dot(second_low, w_up, preferred_element_type=jnp.float32)
    hidden_f32, hidden_back = jax.vjp(swiglu, gate_vals, up_vals)
    hidden_low = hidden_f32.astype(jnp.bfloat16)
    top_grad = upstream.astype(jnp.float32) * live_rows
    top_low = top_grad.astype(jnp.bfloat16)
    grad_hidden = right_trans(top_low, w_down)
    grad_gate_vals, grad_up_vals = hidden_back(grad_hidden)
    gate_low = grad_gate_vals.astype(jnp.bfloat16)
    up_low = grad_up_vals.astype(jnp.bfloat16)
    grad_second = right_trans(gate_low, w_gate) + right_trans(up_low, w_up)
    grad_middle_norm, grad_ffn_gain = second_back(grad_second)
    grad_middle = top_grad + grad_middle_norm
    middle_low = grad_middle.astype(jnp.bfloat16)
    grad_mixed = right_trans(middle_low, w_output).astype(jnp.bfloat16)
    grad_mixed = grad_mixed.reshape(row_count, KV_HEADS, group_size, HEAD_DIM)
    grad_probs = jnp.einsum(
        "qhgd,khd->hgqk", grad_mixed, value_heads, preferred_element_type=jnp.float32
    )
    grad_value_heads = jnp.einsum(
        "hgqk,qhgd->khd", probs_low, grad_mixed, preferred_element_type=jnp.float32
    )
    row_inner = jnp.sum(probs_f32 * grad_probs, axis=-1, keepdims=True)
    grad_scores = (probs_f32 * (grad_probs - row_inner)).astype(jnp.bfloat16)
    grad_query_rot = (
        jnp.einsum("hgqk,khd->qhgd", grad_scores, key_rot, preferred_element_type=jnp.float32)
        * score_scale
    )
    grad_key_rot = (
        jnp.einsum("hgqk,qhgd->khd", grad_scores, grouped, preferred_element_type=jnp.float32)
        * score_scale
    )
    grad_query_raw = rotate(
        grad_query_rot.reshape(row_count, HEADS, HEAD_DIM), cosine_table, -sine_table
    )
    grad_query_raw = grad_query_raw.reshape(row_count, HEADS * HEAD_DIM).astype(jnp.bfloat16)
    grad_key_raw = (
        rotate(grad_key_rot, cosine_table, -sine_table)
        .reshape(row_count, KV_HEADS * HEAD_DIM)
        .astype(jnp.bfloat16)
    )
    grad_value_raw = grad_value_heads.reshape(row_count, KV_HEADS * HEAD_DIM).astype(jnp.bfloat16)
    grad_normed = right_trans(grad_query_raw, w_query)
    grad_normed = grad_normed + right_trans(grad_key_raw, w_key)
    grad_normed = grad_normed + right_trans(grad_value_raw, w_value)
    grad_rows_norm, grad_attn_gain = first_back(grad_normed)
    grad_rows = grad_middle + grad_rows_norm
    operands = (
        normed_low,
        grad_query_raw,
        grad_key_raw,
        grad_value_raw,
        mixed_low,
        middle_low,
        second_low,
        gate_low,
        up_low,
        hidden_low,
        top_low,
    )
    return (grad_rows.astype(jnp.bfloat16), (grad_attn_gain, grad_ffn_gain), operands)


def weight_grads(operands):
    (
        normed_low,
        grad_query_raw,
        grad_key_raw,
        grad_value_raw,
        mixed_low,
        middle_low,
        second_low,
        gate_low,
        up_low,
        hidden_low,
        top_low,
    ) = operands
    return (
        cross_rows(normed_low, grad_query_raw),
        cross_rows(normed_low, grad_key_raw),
        cross_rows(normed_low, grad_value_raw),
        cross_rows(mixed_low, middle_low),
        cross_rows(second_low, gate_low),
        cross_rows(second_low, up_low),
        cross_rows(hidden_low, top_low),
    )


def flat_grads(grads, owner_count):
    pieces = [grad.reshape(owner_count, -1) for grad in grads]
    joined = jnp.concatenate(pieces, axis=1)
    width = joined.shape[1]
    padded = (width + 127) // 128 * 128
    return jnp.pad(joined, ((0, 0), (0, padded - width)))


def unflat_grads(flat_row, shard_shapes):
    flat_row = flat_row.reshape(-1)
    results = []
    offset = 0
    for shape in shard_shapes:
        length = 1
        for extent in shape:
            length = length * extent
        results.append(flat_row[offset : offset + length].reshape(shape))
        offset = offset + length
    return tuple(results)


def store_slot(buffer, rows_new, slot_idx, active):
    current = lax.dynamic_index_in_dim(buffer, slot_idx, 0, keepdims=False)
    chosen = jnp.where(active, rows_new, current)
    return lax.dynamic_update_index_in_dim(buffer, chosen, slot_idx, 0)


def body(
    inputs,
    starts,
    cotangent,
    w_query,
    w_key,
    w_value,
    w_output,
    w_gate,
    w_up,
    w_down,
    attn_gain,
    ffn_gain,
):
    section_idx = lax.axis_index("section")
    section_count = lax.axis_size("section")
    owner_count = lax.axis_size("dp")
    last_section = section_count - 1
    micro_count = inputs.shape[0]
    tick_count = micro_count + section_count - 1
    shard_list = (w_query, w_key, w_value, w_output, w_gate, w_up, w_down, attn_gain, ffn_gain)
    shard_shapes = tuple((piece.shape for piece in shard_list))
    gathered = (
        lax.all_gather(w_query, "dp", axis=1, tiled=True),
        lax.all_gather(w_key, "dp", axis=1, tiled=True),
        lax.all_gather(w_value, "dp", axis=1, tiled=True),
        lax.all_gather(w_output, "dp", axis=1, tiled=True),
        lax.all_gather(w_gate, "dp", axis=1, tiled=True),
        lax.all_gather(w_up, "dp", axis=1, tiled=True),
        lax.all_gather(w_down, "dp", axis=1, tiled=True),
        lax.all_gather(attn_gain, "dp", axis=1, tiled=True),
        lax.all_gather(ffn_gain, "dp", axis=1, tiled=True),
    )
    weights = tuple((piece[0] for piece in gathered))
    blank_rows = jnp.zeros(inputs.shape[1:], jnp.bfloat16)
    kept_in = jnp.zeros(inputs.shape, jnp.bfloat16)
    section_acts = jnp.zeros(inputs.shape, jnp.bfloat16)
    received = blank_rows
    for moment in range(tick_count):
        slot_raw = moment - section_idx
        active = (slot_raw >= 0) & (slot_raw < micro_count)
        slot_idx = jnp.clip(slot_raw, 0, micro_count - 1)
        feed_rows = jnp.where(section_idx == 0, inputs[min(moment, micro_count - 1)], received)
        starts_now = starts[slot_idx]
        produced = lax.cond(
            active, partial(layer_forward, feed_rows, weights, starts_now), lambda: blank_rows
        )
        kept_in = store_slot(kept_in, feed_rows, slot_idx, active)
        section_acts = store_slot(section_acts, produced, slot_idx, active)
        if moment + 1 < tick_count:
            received = from_behind(produced, "section", 1)
    regathered = (
        lax.all_gather(w_query, "dp", axis=1, tiled=True),
        lax.all_gather(w_key, "dp", axis=1, tiled=True),
        lax.all_gather(w_value, "dp", axis=1, tiled=True),
        lax.all_gather(w_output, "dp", axis=1, tiled=True),
        lax.all_gather(w_gate, "dp", axis=1, tiled=True),
        lax.all_gather(w_up, "dp", axis=1, tiled=True),
        lax.all_gather(w_down, "dp", axis=1, tiled=True),
        lax.all_gather(attn_gain, "dp", axis=1, tiled=True),
        lax.all_gather(ffn_gain, "dp", axis=1, tiled=True),
    )
    back_weights = tuple((piece[0] for piece in regathered))
    row_count = inputs.shape[1]
    operand_widths = (D, QD, KVD, KVD, QD, D, D, FF, FF, FF, D)
    blank_operands = tuple(
        (jnp.zeros((row_count, width), jnp.bfloat16) for width in operand_widths)
    )
    blank_gains = (
        jnp.zeros(back_weights[7].shape, jnp.float32),
        jnp.zeros(back_weights[8].shape, jnp.float32),
    )
    operand_store = tuple(
        (jnp.zeros((micro_count, row_count, width), jnp.bfloat16) for width in operand_widths)
    )
    gain_totals = blank_gains
    shard_totals = tuple((jnp.zeros(shape, jnp.float32) for shape in shard_shapes))
    input_grads = jnp.zeros(inputs.shape, jnp.bfloat16)
    returned = blank_rows
    for moment in range(tick_count):
        slot_raw = moment - (last_section - section_idx)
        active = (slot_raw >= 0) & (slot_raw < micro_count)
        slot_idx = jnp.clip(slot_raw, 0, micro_count - 1)
        upstream = jnp.where(
            section_idx == last_section, cotangent[min(moment, micro_count - 1)], returned
        )
        source = lax.dynamic_index_in_dim(kept_in, slot_idx, 0, keepdims=False)
        starts_now = starts[slot_idx]

        def run_keep():
            return layer_backward(source, back_weights, starts_now, upstream)

        def skip_keep():
            return (blank_rows, blank_gains, blank_operands)

        grad_rows, gain_grads, operands = lax.cond(active, run_keep, skip_keep)
        gain_totals = tuple(
            (old_sum + new_sum for old_sum, new_sum in zip(gain_totals, gain_grads))
        )
        operand_store = tuple(
            (
                store_slot(buffer, member, slot_idx, active)
                for buffer, member in zip(operand_store, operands)
            )
        )
        input_grads = store_slot(input_grads, grad_rows, slot_idx, active)
        if moment + 1 < tick_count:
            returned = from_behind(grad_rows, "section", -1)
    totals = weight_grads(operand_store) + gain_totals
    scattered = lax.psum_scatter(
        flat_grads(totals, owner_count), "dp", scatter_dimension=0, tiled=True
    )
    shard_totals = unflat_grads(scattered, shard_shapes)
    return (section_acts[None], input_grads[None]) + tuple(shard_totals)


def solution(mesh):
    return jax.shard_map(
        body,
        mesh=mesh,
        in_specs=(
            P(None, "dp", None),
            P(None, "dp"),
            P(None, "dp", None),
            P("section", "dp", None),
            P("section", "dp", None),
            P("section", "dp", None),
            P("section", "dp", None),
            P("section", "dp", None),
            P("section", "dp", None),
            P("section", "dp", None),
            P("section", "dp"),
            P("section", "dp"),
        ),
        out_specs=(
            P("section", None, "dp", None),
            P("section", None, "dp", None),
            P("section", "dp", None),
            P("section", "dp", None),
            P("section", "dp", None),
            P("section", "dp", None),
            P("section", "dp", None),
            P("section", "dp", None),
            P("section", "dp", None),
            P("section", "dp"),
            P("section", "dp"),
        ),
        check_vma=False,
    )
```

profile of v0, /device:TPU:0, one launch (start us, length us, event | category | flops | bytes accessed | tf_op | source)
XLA Modules:
  0.0 1488.7 jit_solution(15037251605952661277)
XLA Ops:
  15.2 188.1 %all_gather.37 = bf16[1,960,320]{2,0,1:T(2,128)(2,1)S(1)} all-gather(bf16[1,15,320]{2,0,1:T(2,128)(2,1)S(1)} %copy.462), channel_id=1, replica_groups=mesh['section'=2,'dp'=64] {'dp'}, dimensions={1}, use_global_device_ids=true | all-gather | bytes 624000 | tf_op jit(solution)/shard_map/all_gather | solution.py:276
  206.3 183.7 %all_gather.38 = bf16[1,960,320]{2,0,1:T(2,128)(2,1)S(1)} all-gather(bf16[1,15,320]{2,0,1:T(2,128)(2,1)S(1)} %copy.464), channel_id=1, replica_groups=mesh['section'=2,'dp'=64] {'dp'}, dimensions={1}, use_global_device_ids=true | all-gather | bytes 624000 | tf_op jit(solution)/shard_map/all_gather | solution.py:275
  394.3 173.6 %all-reduce.4 = (bf16[960]{0:T(1024)(128)(2,1)S(1)}, bf16[960]{0:T(1024)(128)(2,1)S(1)}) all-reduce(bf16[960]{0:T(1024)(128)(2,1)S(1)} %dynamic-update-slice, bf16[960]{0:T(1024)(128)(2,1)S(1)} %dynamic-update-slice.1), channel_id=1, replica_groups=mesh['section'=2,'dp'=64] {'dp'}, use_global_device_ids=true, to_apply=%add.1 | all-reduce | flops 1920 | bytes 7680 | tf_op jit(solution)/shard_map/squeeze | solution.py:284
  575.7 7.3 copy.612
  583.0 7.2 copy.611
  590.9 39.5 %conditional.6 = (bf16[64,960]{1,0:T(8,128)(2,1)}) conditional(s32[]{:T(128)} %convert_element_type.647, () %tuple.72, (pred[]{:T(512)}, bf16[1,64,960]{2,1,0:T(8,128)(2,1)}, bf16[64,960]{1,0:T(8,128)(2,1)}, bf16[960]{0:T(1024)(128)(2,1)S(1)}, bf16[960,320]{0,1:T(8,128)(2,1)S(1)}, /*index=5*/s32[2,64]{1,0:T(2,128)S(1)}, s32[]{:T(128)}, ...), branch_computations={%region_0.1_spmd, %region_1.6_spmd} | conditional | flops 1286292992 | bytes 26960564 | solution.py:295
  623.5 6.9 fusion.9
  634.6 39.3 %conditional.7 = (bf16[64,960]{1,0:T(8,128)(2,1)}) conditional(s32[]{:T(128)} %convert_element_type.648, () %tuple.74, (bf16[64,960]{1,0:T(8,128)(2,1)}, bf16[960]{0:T(1024)(128)(2,1)S(1)}, bf16[960,320]{0,1:T(8,128)(2,1)S(1)}, s32[2,64]{1,0:T(2,128)S(1)}, s32[]{:T(128)}, /*index=5*/bf16[960,320]{0,1:T(8,128)(2,1)S(1)}, ...), branch_computations={%region_6.7_spmd, %region_7.12_spmd} | conditional | flops 1286231552 | bytes 26223256 | solution.py:295
  662.8 4.3 fusion.84
  667.1 6.9 fusion.71
  680.9 9.5 conditional.9
  711.4 38.0 %collective-permute-done.2 = bf16[64,960]{1,0:T(8,128)(2,1)} collective-permute-done((bf16[64,960]{1,0:T(8,128)(2,1)}, bf16[64,960]{1,0:T(8,128)(2,1)}, u32[]{:S(2)}, u32[]{:S(2)}) %collective-permute-start.2) | collective-permute-done | bytes 122912 | tf_op jit(solution)/shard_map/ppermute | solution.py:22
  749.4 65.9 %conditional.10 = (bf16[64,960]{1,0:T(8,128)(2,1)}, f32[960]{0:T(1024)}, f32[960]{0:T(1024)}, bf16[64,960]{1,0:T(8,128)(2,1)}, bf16[64,320]{0,1:T(8,128)(2,1)}, ...) conditional(s32[]{:T(128)} %convert_element_type.651, () %tuple.80, ...), branch_computations={%region_29.30_spmd, %region_30.40_spmd} | conditional | flops 2275088896 | bytes 119995208 | solution.py:346
  855.5 65.6 %conditional.11 = (bf16[64,960]{1,0:T(8,128)(2,1)}, f32[960]{0:T(1024)}, f32[960]{0:T(1024)}, bf16[64,960]{1,0:T(8,128)(2,1)}, bf16[64,320]{0,1:T(8,128)(2,1)}, ...) conditional(s32[]{:T(128)} %convert_element_type.652, () %tuple.82, ...), branch_computations={%region_40.41_spmd, %region_41.51_spmd} | conditional | flops 2275088896 | bytes 119995208 | solution.py:346
  928.1 5.3 reshape.1296
  948.8 5.4 reshape.1299
  956.9 6.1 convolution_bitcast_fusion.11
  963.0 11.9 reshape.1300
  976.0 6.1 convolution_bitcast_fusion.10
  982.1 12.0 reshape.1301
  996.1 5.5 convolution_bitcast_fusion.9
  1001.6 12.2 reshape.1302
  1014.9 11.4 dynamic-update-slice.2
  1026.3 6.4 dynamic-update-slice.3
  1032.7 6.2 dynamic-update-slice.4
  1039.0 12.3 dynamic-update-slice.5
  1051.3 8.6 constant_dynamic-update-slice_fusion.8
  1059.9 4.3 constant_dynamic-update-slice_fusion.7
  1064.3 8.3 constant_dynamic-update-slice_fusion.6
  1075.4 27.2 %pad.4 = f32[64,153728]{1,0:T(8,128)} pad(f32[64,153630]{1,0:T(8,128)} %dynamic-update-slice.10, f32[]{:T(128)} %constant.520.clone.1), padding=0_0x0_98 | pad | bytes 78683648 | tf_op jit(solution)/shard_map/jit(_pad)/pad | solution.py:229
  1107.5 360.2 %all-reduce.7.cloned.1.call-done = f32[64,153728]{1,0:T(8,128)} async-done(((f32[64,153728]{1,0:T(8,128)}), f32[64,153728]{1,0:T(8,128)}) %all-reduce.7.cloned.1.call-update) | async-done | bytes 39354384
  1474.5 4.4 dynamic-slice_reduce_fusion
  (568 shorter events, 341.1 us)
Async XLA Ops:
  7.2 385.2 %copy-start.120 = (u32[128]{0:T(128)S(1)}, u32[128]{0:T(128)}, u32[]{:S(2)}) copy-start(u32[128]{0:T(128)} %constant.534) | copy-start | bytes 1540
  7.2 386.6 %copy-start.126 = (bf16[1,15]{1,0:T(2,128)(2,1)S(1)}, bf16[1,15]{1,0:T(2,128)(2,1)}, u32[]{:S(2)}) copy-start(bf16[1,15]{1,0:T(2,128)(2,1)} %param.34) | copy-start | bytes 94
  7.2 386.9 %copy-start.127 = (bf16[1,15]{1,0:T(2,128)(2,1)S(1)}, bf16[1,15]{1,0:T(2,128)(2,1)}, u32[]{:S(2)}) copy-start(bf16[1,15]{1,0:T(2,128)(2,1)} %param.35) | copy-start | bytes 94
  7.2 560.7 %copy-start.70 = (bf16[2,64,960]{2,1,0:T(8,128)(2,1)S(1)}, bf16[2,64,960]{2,1,0:T(8,128)(2,1)}, u32[]{:S(2)}) copy-start(bf16[2,64,960]{2,1,0:T(8,128)(2,1)} %param.24) | copy-start | bytes 737284
  7.2 561.4 %all-gather.6.cloned.1.call-start = ((), (), s32[]{:S(2)}) async-start(), calls=%async_computation | async-start | bytes 3993600 | tf_op jit(solution)/shard_map/all_gather | solution.py:274
  8.8 562.8 %all-gather.8.cloned.1.call-start = ((), (), s32[]{:S(2)}) async-start(), calls=%async_computation.1 | async-start | bytes 3993600 | tf_op jit(solution)/shard_map/all_gather | solution.py:277
  10.3 565.5 %all-gather.10.cloned.1.call-start = ((), (), s32[]{:S(2)}) async-start(), calls=%async_computation.2 | async-start | bytes 9984000 | tf_op jit(solution)/shard_map/all_gather | solution.py:278
  12.0 571.0 %all-gather.12.cloned.1.call-start = ((), (), s32[]{:S(2)}) async-start(), calls=%async_computation.3 | async-start | bytes 9984000 | tf_op jit(solution)/shard_map/all_gather | solution.py:279
  13.8 576.5 %all-gather.14.cloned.1.call-start = ((), (), s32[]{:S(2)}) async-start(), calls=%async_computation.4 | async-start | bytes 5324800 | tf_op jit(solution)/shard_map/all_gather | solution.py:280
  14.4 1453.3 %all-reduce.7.cloned.1.call-start = ((), (), s32[]{:S(2)}) async-start(), calls=%async_computation.5 | async-start | bytes 78708736
  205.6 474.7 %copy-start.4 = (bf16[1,960,320]{1,2,0:T(8,128)(2,1)}, bf16[1,960,320]{1,2,0:T(8,128)(2,1)S(1)}, u32[]{:S(2)}) copy-start(bf16[1,960,320]{1,2,0:T(8,128)(2,1)S(1)} %copy.463) | copy-start | bytes 1843204
  392.4 287.9 %copy-start.14 = (bf16[1,960,320]{1,2,0:T(8,128)(2,1)}, bf16[1,960,320]{1,2,0:T(8,128)(2,1)S(1)}, u32[]{:S(2)}) copy-start(bf16[1,960,320]{1,2,0:T(8,128)(2,1)S(1)} %copy.465) | copy-start | bytes 1843204
  567.9 112.4 %copy-start.94 = (bf16[960]{0:T(1024)(128)(2,1)}, bf16[960]{0:T(1024)(128)(2,1)S(1)}, u32[]{:S(2)}) copy-start(bf16[960]{0:T(1024)(128)(2,1)S(1)} %get-tuple-element.1183) | copy-start | bytes 5764
  567.9 112.4 %copy-start.98 = (bf16[960]{0:T(1024)(128)(2,1)}, bf16[960]{0:T(1024)(128)(2,1)S(1)}, u32[]{:S(2)}) copy-start(bf16[960]{0:T(1024)(128)(2,1)S(1)} %get-tuple-element.1184) | copy-start | bytes 5764
  630.4 2.6 collective-permute-start
  674.0 4.6 collective-permute-start.1
  690.4 59.0 %collective-permute-start.2 = (bf16[64,960]{1,0:T(8,128)(2,1)}, bf16[64,960]{1,0:T(8,128)(2,1)}, u32[]{:S(2)}, u32[]{:S(2)}) collective-permute-start(bf16[64,960]{1,0:T(8,128)(2,1)} %get-tuple-element.623), channel_id=1, source_target_pairs={{64,0},{65,1},{66,2},{67,3},{68,4},{69,5},{70,6},{71,7},{72,8},{73... | collective-permute-start | bytes 368648 | tf_op jit(solution)/shard_map/ppermute | solution.py:22
  695.4 54.0 %copy-start.5 = (bf16[1,960,320]{1,2,0:T(8,128)(2,1)S(1)}, bf16[1,960,320]{1,2,0:T(8,128)(2,1)}, u32[]{:S(2)}) copy-start(bf16[1,960,320]{1,2,0:T(8,128)(2,1)} %copy-done.4) | copy-start | bytes 1843204
  695.4 54.0 %copy-start.15 = (bf16[1,960,320]{1,2,0:T(8,128)(2,1)S(1)}, bf16[1,960,320]{1,2,0:T(8,128)(2,1)}, u32[]{:S(2)}) copy-start(bf16[1,960,320]{1,2,0:T(8,128)(2,1)} %copy-done.14) | copy-start | bytes 1843204
  695.4 54.0 %copy-start.95 = (bf16[960]{0:T(1024)(128)(2,1)S(1)}, bf16[960]{0:T(1024)(128)(2,1)}, u32[]{:S(2)}) copy-start(bf16[960]{0:T(1024)(128)(2,1)} %copy-done.94) | copy-start | bytes 5764
  695.4 54.0 %copy-start.108 = (s32[2,64]{1,0:T(2,128)S(1)}, s32[2,64]{1,0:T(2,128)}, u32[]{:S(2)}) copy-start(s32[2,64]{1,0:T(2,128)} %param.25) | copy-start | bytes 1540
  749.4 15.7 %copy-start.10 = (bf16[960,320]{0,1:T(8,128)(2,1)}, bf16[960,320]{0,1:T(8,128)(2,1)S(1)}, u32[]{:S(2)}) copy-start(bf16[960,320]{0,1:T(8,128)(2,1)S(1)} %get-tuple-element.1128) | copy-start | bytes 1843204 | tf_op jit(solution)/shard_map/cond
  749.4 15.7 %copy-start.20 = (bf16[960,320]{0,1:T(8,128)(2,1)}, bf16[960,320]{0,1:T(8,128)(2,1)S(1)}, u32[]{:S(2)}) copy-start(bf16[960,320]{0,1:T(8,128)(2,1)S(1)} %get-tuple-element.549) | copy-start | bytes 1843204 | tf_op jit(solution)/shard_map/cond
  815.3 40.1 %collective-permute-start.3 = (bf16[64,960]{1,0:T(8,128)(2,1)}, bf16[64,960]{1,0:T(8,128)(2,1)}, u32[]{:S(2)}, u32[]{:S(2)}) collective-permute-start(bf16[64,960]{1,0:T(8,128)(2,1)} %get-tuple-element.624), channel_id=1, source_target_pairs={{64,0},{65,1},{66,2},{67,3},{68,4},{69,5},{70,6},{71,7},{72,8},{73... | collective-permute-start | bytes 368648 | tf_op jit(solution)/shard_map/ppermute | solution.py:22
  818.5 37.0 %copy-start.6 = (bf16[1,960,320]{1,2,0:T(8,128)(2,1)S(1)}, bf16[1,960,320]{1,2,0:T(8,128)(2,1)}, u32[]{:S(2)}) copy-start(bf16[1,960,320]{1,2,0:T(8,128)(2,1)} %copy-done.4) | copy-start | bytes 1843204
  818.5 37.0 %copy-start.16 = (bf16[1,960,320]{1,2,0:T(8,128)(2,1)S(1)}, bf16[1,960,320]{1,2,0:T(8,128)(2,1)}, u32[]{:S(2)}) copy-start(bf16[1,960,320]{1,2,0:T(8,128)(2,1)} %copy-done.14) | copy-start | bytes 1843204
  818.5 37.0 %copy-start.96 = (bf16[960]{0:T(1024)(128)(2,1)S(1)}, bf16[960]{0:T(1024)(128)(2,1)}, u32[]{:S(2)}) copy-start(bf16[960]{0:T(1024)(128)(2,1)} %copy-done.94) | copy-start | bytes 5764
  818.5 37.0 %copy-start.109 = (s32[2,64]{1,0:T(2,128)S(1)}, s32[2,64]{1,0:T(2,128)}, u32[]{:S(2)}) copy-start(s32[2,64]{1,0:T(2,128)} %param.25) | copy-start | bytes 1540
  832.3 17.9 %copy-start.68 = (bf16[2,64,320]{2,1,0:T(8,128)(2,1)S(1)}, bf16[2,64,320]{2,1,0:T(8,128)(2,1)}, u32[]{:S(2)}) copy-start(bf16[2,64,320]{2,1,0:T(8,128)(2,1)} %constant_dynamic-update-slice_fusion.1) | copy-start | bytes 245764
  855.5 15.3 %copy-start.12 = (bf16[960,320]{0,1:T(8,128)(2,1)}, bf16[960,320]{0,1:T(8,128)(2,1)S(1)}, u32[]{:S(2)}) copy-start(bf16[960,320]{0,1:T(8,128)(2,1)S(1)} %get-tuple-element.1143) | copy-start | bytes 1843204 | tf_op jit(solution)/shard_map/cond
  1039.0 20.9 %slice-start.18 = ((s8[9830400]{0:T(1024)(128)(4,1)}), s8[1441792]{0:T(1024)(128)(4,1)S(1)}, s32[]{:S(2)}) async-start(s8[9830400]{0:T(1024)(128)(4,1)} %bitcast.940), calls=%async_computation.24 | async-start | bytes 2883584
  1107.5 374.1 %copy-start.83 = (bf16[1,2,64,960]{3,2,1,0:T(8,128)(2,1)}, bf16[1,2,64,960]{3,2,1,0:T(8,128)(2,1)S(1)}, u32[]{:S(2)}) copy-start(bf16[1,2,64,960]{3,2,1,0:T(8,128)(2,1)S(1)} %get-tuple-element.1332) | copy-start | bytes 737284
  (98 other events, 546.2 us)
Sparse Core Ops, SparseCore 0:
  11.4 71.4 all-gather.5
  86.2 67.3 all-gather.7
  157.0 83.9 all-gather.9
  244.3 85.3 all-gather.11
  332.5 69.7 all-gather.13
  1102.8 364.8 all-reduce.6
where the time goes:
time: 1500 us; the launch traced here: 1490 us
  blocking collectives  545 us (36%)
  waiting for transfers between devices  400 us (27%)
  local copies, waits for them, and re-layouts  291 us (19%)
  matrix products  152 us (10%)
  other arithmetic  75 us (5%)
  between operations  15.9 us (1%)
    unnamed x7, waiting for transfers between devices  361 us
    all_gather x1, blocking collectives, body(): lax.all_gather(w_value, 'dp', axis=1, tiled=True)  188 us
    all_gather x1, blocking collectives, body(): lax.all_gather(w_key, 'dp', axis=1, tiled=True)  184 us
    squeeze x1, blocking collectives, body(): weights = tuple((piece[0] for piece in gathered))  174 us
    unnamed x147, local copies, waits for them, and re-layouts  94.3 us
    reshape x9, local copies, waits for them, and re-layouts, flat_grads(): pieces = [grad.reshape(owner_count, -1) for grad in grads]  52.9 us
    ppermute x4, waiting for transfers between devices, from_behind(): lax.ppermute(value, axis, [(source, source + steps) for source in range(f...  38.7 us
    dynamic_slice x30, local copies, waits for them, and re-layouts, store_slot(): current = lax.dynamic_index_in_dim(buffer, slot_idx, 0, keepdims=False)  31.6 us
  transfers between devices with their start and end apart: 10, of which 3 were waited for; matrix products, arithmetic and copies ran while one was open for 6% of the time, Pallas kernels for 0%

commit v1 on v0

--- a/solution.py
+++ b/solution.py
@@ -14,6 +14,12 @@
 norm_eps = 1e-05
 masked_score = -1e30
 rope_base = 10000.0
+
+
+def gather_from_all(x, axis, dim):
+    size = lax.axis_size(axis)
+    repeats = [size if d == dim else 1 for d in range(x.ndim)]
+    return lax.all_to_all(jnp.tile(x, repeats), axis, split_axis=dim, concat_axis=dim, tiled=True)
 
 
 def from_behind(value, axis, steps):
@@ -272,7 +278,7 @@
     shard_shapes = tuple((piece.shape for piece in shard_list))
     gathered = (
         lax.all_gather(w_query, "dp", axis=1, tiled=True),
-        lax.all_gather(w_key, "dp", axis=1, tiled=True),
+        gather_from_all(w_key, "dp", 1),
         lax.all_gather(w_value, "dp", axis=1, tiled=True),
         lax.all_gather(w_output, "dp", axis=1, tiled=True),
         lax.all_gather(w_gate, "dp", axis=1, tiled=True),

time: 1500 us -> 1530 us (1.020)
  blocking collectives: 545 us -> 565 us
    all_gather x1, blocking collectives: 184 us -> 203 us  [body(): lax.all_gather(w_key, 'dp', axis=1, tiled=True)]
    unnamed x147 -> x152, local copies, waits for them, and re-layouts: 94.3 us -> 96.7 us
  transfers between devices with their start and end apart: 10 -> 11, of which waited for: 3 -> 2; matrix products, arithmetic and copies ran while one was open for 6% -> 7% of each run, Pallas kernels for 0% -> 0%
where the time goes in v1:
time: 1530 us; the launch traced here: 1510 us
  blocking collectives  565 us (37%)
  waiting for transfers between devices  393 us (26%)
  local copies, waits for them, and re-layouts  293 us (19%)
  matrix products  152 us (10%)
  other arithmetic  75.1 us (5%)
  starting transfers between devices  17.7 us (1%)
  between operations  16.1 us (1%)
    unnamed x7, waiting for transfers between devices  360 us
    all_gather x1, blocking collectives, body(): lax.all_gather(w_key, 'dp', axis=1, tiled=True)  203 us
    all_gather x1, blocking collectives, body(): lax.all_gather(w_value, 'dp', axis=1, tiled=True)  189 us
    squeeze x1, blocking collectives, body(): weights = tuple((piece[0] for piece in gathered))  173 us
    unnamed x152, local copies, waits for them, and re-layouts  96.7 us
    reshape x9, local copies, waits for them, and re-layouts, flat_grads(): pieces = [grad.reshape(owner_count, -1) for grad in grads]  52.9 us
    ppermute x4, waiting for transfers between devices, from_behind(): lax.ppermute(value, axis, [(source, source + steps) for source in range(f...  32.8 us
    dynamic_slice x30, local copies, waits for them, and re-layouts, store_slot(): current = lax.dynamic_index_in_dim(buffer, slot_idx, 0, keepdims=False)  30.8 us
  transfers between devices with their start and end apart: 11, of which 2 were waited for; matrix products, arithmetic and copies ran while one was open for 7% of the time, Pallas kernels for 0%

profile of v1, /device:TPU:0, one launch (start us, length us, event | category | flops | bytes accessed | tf_op | source)
XLA Modules:
  0.0 1513.0 jit_solution(13037895778211483063)
XLA Ops:
  16.1 5.4 reduce.10
  23.6 11.5 all-to-all-start
  35.8 189.2 %all_gather.36 = bf16[1,960,320]{2,0,1:T(2,128)(2,1)S(1)} all-gather(bf16[1,15,320]{2,0,1:T(2,128)(2,1)S(1)} %copy.454), channel_id=1, replica_groups=mesh['section'=2,'dp'=64] {'dp'}, dimensions={1}, use_global_device_ids=true | all-gather | bytes 624000 | tf_op jit(solution)/shard_map/all_gather | solution.py:282
  229.3 173.2 %all-reduce.4 = (bf16[960]{0:T(1024)(128)(2,1)S(1)}, bf16[960]{0:T(1024)(128)(2,1)S(1)}) all-reduce(bf16[960]{0:T(1024)(128)(2,1)S(1)} %dynamic-update-slice, bf16[960]{0:T(1024)(128)(2,1)S(1)} %dynamic-update-slice.1), channel_id=1, replica_groups=mesh['section'=2,'dp'=64] {'dp'}, use_global_device_ids=true, to_apply=%add.1 | all-reduce | flops 1920 | bytes 7680 | tf_op jit(solution)/shard_map/squeeze | solution.py:290
  414.5 7.3 copy.606
  421.7 7.2 copy.605
  429.7 38.8 %conditional.6 = (bf16[64,960]{1,0:T(8,128)(2,1)}) conditional(s32[]{:T(128)} %convert_element_type.647, () %tuple.72, (pred[]{:T(512)}, bf16[1,64,960]{2,1,0:T(8,128)(2,1)}, bf16[64,960]{1,0:T(8,128)(2,1)}, bf16[960]{0:T(1024)(128)(2,1)S(1)}, bf16[960,320]{0,1:T(8,128)(2,1)S(1)}, /*index=5*/s32[2,64]{1,0:T(2,128)S(1)}, s32[]{:T(128)}, ...), branch_computations={%region_0.1_spmd, %region_1.6_spmd} | conditional | flops 1286292992 | bytes 26960564 | solution.py:301
  461.5 6.9 fusion.9
  470.4 202.9 %all_gather.43 = bf16[1,960,320]{2,0,1:T(2,128)(2,1)} all-gather(bf16[1,15,320]{2,0,1:T(2,128)(2,1)} %copy.468), channel_id=1, replica_groups=mesh['section'=2,'dp'=64] {'dp'}, dimensions={1}, use_global_device_ids=true | all-gather | bytes 624000 | tf_op jit(solution)/shard_map/all_gather | solution.py:310
  675.0 31.9 %conditional.7 = (bf16[64,960]{1,0:T(8,128)(2,1)}) conditional(s32[]{:T(128)} %convert_element_type.648, () %tuple.74, (bf16[64,960]{1,0:T(8,128)(2,1)}, bf16[960]{0:T(1024)(128)(2,1)S(1)}, bf16[960,320]{0,1:T(8,128)(2,1)S(1)}, s32[2,64]{1,0:T(2,128)S(1)}, s32[]{:T(128)}, /*index=5*/bf16[960,320]{0,1:T(8,128)(2,1)S(1)}, ...), branch_computations={%region_6.7_spmd, %region_7.12_spmd} | conditional | flops 1286231552 | bytes 26714804 | solution.py:301
  700.2 6.7 fusion.71
  709.7 4.6 copy.469
  716.6 9.3 conditional.9
  744.0 32.8 %collective-permute-done.2 = bf16[64,960]{1,0:T(8,128)(2,1)} collective-permute-done((bf16[64,960]{1,0:T(8,128)(2,1)}, bf16[64,960]{1,0:T(8,128)(2,1)}, u32[]{:S(2)}, u32[]{:S(2)}) %collective-permute-start.2) | collective-permute-done | bytes 122912 | tf_op jit(solution)/shard_map/ppermute | solution.py:28
  776.9 64.6 %conditional.10 = (bf16[64,960]{1,0:T(8,128)(2,1)}, f32[960]{0:T(1024)}, f32[960]{0:T(1024)}, bf16[64,960]{1,0:T(8,128)(2,1)}, bf16[64,320]{0,1:T(8,128)(2,1)}, ...) conditional(s32[]{:T(128)} %convert_element_type.651, () %tuple.80, ...), branch_computations={%region_29.30_spmd, %region_30.40_spmd} | conditional | flops 2275088896 | bytes 115481488 | solution.py:352
  880.7 64.5 %conditional.11 = (bf16[64,960]{1,0:T(8,128)(2,1)}, f32[960]{0:T(1024)}, f32[960]{0:T(1024)}, bf16[64,960]{1,0:T(8,128)(2,1)}, bf16[64,320]{0,1:T(8,128)(2,1)}, ...) conditional(s32[]{:T(128)} %convert_element_type.652, () %tuple.82, ...), branch_computations={%region_40.41_spmd, %region_41.51_spmd} | conditional | flops 2275088896 | bytes 115481488 | solution.py:352
  952.2 5.3 reshape.1302
  973.0 5.4 reshape.1305
  981.0 6.1 convolution_bitcast_fusion.11
  987.1 12.0 reshape.1306
  1000.2 6.1 convolution_bitcast_fusion.10
  1006.3 12.0 reshape.1307
  1020.3 5.5 convolution_bitcast_fusion.9
  1025.8 12.2 reshape.1308
  1039.1 11.4 dynamic-update-slice.2
  1050.5 6.5 dynamic-update-slice.3
  1057.0 6.3 dynamic-update-slice.4
  1063.3 12.3 dynamic-update-slice.5
  1075.6 8.6 constant_dynamic-update-slice_fusion.8
  1088.5 8.4 constant_dynamic-update-slice_fusion.6
  1099.7 27.1 %pad.4 = f32[64,153728]{1,0:T(8,128)} pad(f32[64,153630]{1,0:T(8,128)} %dynamic-update-slice.10, f32[]{:T(128)} %constant.520.clone.1), padding=0_0x0_98 | pad | bytes 78683648 | tf_op jit(solution)/shard_map/jit(_pad)/pad | solution.py:235
  1132.4 359.4 %all-reduce.7.cloned.1.call-done = f32[64,153728]{1,0:T(8,128)} async-done(((f32[64,153728]{1,0:T(8,128)}), f32[64,153728]{1,0:T(8,128)}) %all-reduce.7.cloned.1.call-update) | async-done | bytes 39354384
  (589 shorter events, 343.1 us)
Async XLA Ops:
  7.2 28.0 %copy-start.97 = (bf16[1,15,320]{2,1,0:T(8,128)(2,1)S(1)}, bf16[1,15,320]{2,1,0:T(8,128)(2,1)}, u32[]{:S(2)}) copy-start(bf16[1,15,320]{2,1,0:T(8,128)(2,1)} %param.28) | copy-start | bytes 28804
  7.2 28.6 %copy-start.104 = (bf16[1,15,320]{2,1,0:T(8,128)(2,1)S(1)}, bf16[1,15,320]{2,1,0:T(8,128)(2,1)}, u32[]{:S(2)}) copy-start(bf16[1,15,320]{2,1,0:T(8,128)(2,1)} %param.29) | copy-start | bytes 28804
  7.2 399.9 %all-gather.6.cloned.1.call-start = ((), (), s32[]{:S(2)}) async-start(), calls=%async_computation.1 | async-start | bytes 3993600 | tf_op jit(solution)/shard_map/all_gather | solution.py:280
  8.7 401.5 %all-gather.8.cloned.1.call-start = ((), (), s32[]{:S(2)}) async-start(), calls=%async_computation.2 | async-start | bytes 3993600 | tf_op jit(solution)/shard_map/all_gather | solution.py:283
  10.2 404.2 %all-gather.10.cloned.1.call-start = ((), (), s32[]{:S(2)}) async-start(), calls=%async_computation.3 | async-start | bytes 9984000 | tf_op jit(solution)/shard_map/all_gather | solution.py:284
  12.0 409.8 %all-gather.12.cloned.1.call-start = ((), (), s32[]{:S(2)}) async-start(), calls=%async_computation.4 | async-start | bytes 9984000 | tf_op jit(solution)/shard_map/all_gather | solution.py:285
  13.7 415.3 %all-gather.14.cloned.1.call-start = ((), (), s32[]{:S(2)}) async-start(), calls=%async_computation.5 | async-start | bytes 5324800 | tf_op jit(solution)/shard_map/all_gather | solution.py:286
  15.1 212.3 %copy-start.124 = (u32[128]{0:T(128)S(1)}, u32[128]{0:T(128)}, u32[]{:S(2)}) copy-start(u32[128]{0:T(128)} %constant.534) | copy-start | bytes 1540
  15.1 213.7 %copy-start.132 = (bf16[1,15]{1,0:T(2,128)(2,1)S(1)}, bf16[1,15]{1,0:T(2,128)(2,1)}, u32[]{:S(2)}) copy-start(bf16[1,15]{1,0:T(2,128)(2,1)} %param.34) | copy-start | bytes 94
  15.1 213.9 %copy-start.133 = (bf16[1,15]{1,0:T(2,128)(2,1)S(1)}, bf16[1,15]{1,0:T(2,128)(2,1)}, u32[]{:S(2)}) copy-start(bf16[1,15]{1,0:T(2,128)(2,1)} %param.35) | copy-start | bytes 94
  15.5 386.9 %copy-start.54 = (bf16[2,64,960]{2,1,0:T(8,128)(2,1)S(1)}, bf16[2,64,960]{2,1,0:T(8,128)(2,1)}, u32[]{:S(2)}) copy-start(bf16[2,64,960]{2,1,0:T(8,128)(2,1)} %param.24) | copy-start | bytes 737284
  23.6 379.6 %all-to-all-start = ((bf16[64,2,2400]{2,1,0:T(2,128)(2,1)}), bf16[64,2,2400]{2,1,0:T(2,128)(2,1)S(1)}, u32[]{:S(2)}, u32[]{:S(2)}) async-start(bf16[64,2,2400]{2,1,0:T(2,128)(2,1)} %reshape.1377), calls=%async_computation | async-start | bytes 1245184 | tf_op jit(solution)/shard_map/all_to_all | solution.py:22
  35.1 1456.8 %all-reduce.7.cloned.1.call-start = ((), (), s32[]{:S(2)}) async-start(), calls=%async_computation.6 | async-start | bytes 78708736
  227.4 489.2 %copy-start.4 = (bf16[1,960,320]{1,2,0:T(8,128)(2,1)}, bf16[1,960,320]{1,2,0:T(8,128)(2,1)S(1)}, u32[]{:S(2)}) copy-start(bf16[1,960,320]{1,2,0:T(8,128)(2,1)S(1)} %copy.455) | copy-start | bytes 1843204
  402.5 314.2 %copy-start.90 = (bf16[960]{0:T(1024)(128)(2,1)}, bf16[960]{0:T(1024)(128)(2,1)S(1)}, u32[]{:S(2)}) copy-start(bf16[960]{0:T(1024)(128)(2,1)S(1)} %get-tuple-element.1183) | copy-start | bytes 5764
  402.5 314.2 %copy-start.94 = (bf16[960]{0:T(1024)(128)(2,1)}, bf16[960]{0:T(1024)(128)(2,1)S(1)}, u32[]{:S(2)}) copy-start(bf16[960]{0:T(1024)(128)(2,1)S(1)} %get-tuple-element.1184) | copy-start | bytes 5764
  407.1 267.9 %copy-start.14 = (bf16[1,960,320]{1,2,0:T(8,128)(2,1)}, bf16[1,960,320]{1,2,0:T(8,128)(2,1)S(1)}, u32[]{:S(2)}) copy-start(bf16[1,960,320]{1,2,0:T(8,128)(2,1)S(1)} %copy.457) | copy-start | bytes 1843204
  468.5 204.9 %collective-permute-start = (bf16[64,960]{1,0:T(8,128)(2,1)}, bf16[64,960]{1,0:T(8,128)(2,1)}, u32[]{:S(2)}, u32[]{:S(2)}) collective-permute-start(bf16[64,960]{1,0:T(8,128)(2,1)} %get-tuple-element.1418), channel_id=1, source_target_pairs={{0,64},{1,65},{2,66},{3,67},{4,68},{5,69},{6,70},{7,71},{8,72},{9,... | collective-permute-start | bytes 368648 | tf_op jit(solution)/shard_map/ppermute | solution.py:28
  706.9 7.5 collective-permute-start.1
  725.9 50.9 %collective-permute-start.2 = (bf16[64,960]{1,0:T(8,128)(2,1)}, bf16[64,960]{1,0:T(8,128)(2,1)}, u32[]{:S(2)}, u32[]{:S(2)}) collective-permute-start(bf16[64,960]{1,0:T(8,128)(2,1)} %get-tuple-element.623), channel_id=1, source_target_pairs={{64,0},{65,1},{66,2},{67,3},{68,4},{69,5},{70,6},{71,7},{72,8},{73... | collective-permute-start | bytes 368648 | tf_op jit(solution)/shard_map/ppermute | solution.py:28
  729.7 47.2 %copy-start.5 = (bf16[1,960,320]{1,2,0:T(8,128)(2,1)S(1)}, bf16[1,960,320]{1,2,0:T(8,128)(2,1)}, u32[]{:S(2)}) copy-start(bf16[1,960,320]{1,2,0:T(8,128)(2,1)} %copy-done.4) | copy-start | bytes 1843204
  729.7 47.2 %copy-start.91 = (bf16[960]{0:T(1024)(128)(2,1)S(1)}, bf16[960]{0:T(1024)(128)(2,1)}, u32[]{:S(2)}) copy-start(bf16[960]{0:T(1024)(128)(2,1)} %copy-done.90) | copy-start | bytes 5764
  729.7 47.2 %copy-start.112 = (s32[2,64]{1,0:T(2,128)S(1)}, s32[2,64]{1,0:T(2,128)}, u32[]{:S(2)}) copy-start(s32[2,64]{1,0:T(2,128)} %param.25) | copy-start | bytes 1540
  734.8 42.1 %copy-start.16 = (bf16[2,64,2560]{2,1,0:T(8,128)(2,1)}, bf16[2,64,2560]{2,1,0:T(8,128)(2,1)S(1)}, u32[]{:S(2)}) copy-start(bf16[2,64,2560]{2,1,0:T(8,128)(2,1)S(1)} %bitcast_dynamic-update-slice_fusion.2) | copy-start | bytes 1966084
  841.5 29.1 %copy-start.17 = (bf16[2,64,2560]{2,1,0:T(8,128)(2,1)S(1)}, bf16[2,64,2560]{2,1,0:T(8,128)(2,1)}, u32[]{:S(2)}) copy-start(bf16[2,64,2560]{2,1,0:T(8,128)(2,1)} %copy-done.16) | copy-start | bytes 1966084
  841.5 39.2 %collective-permute-start.3 = (bf16[64,960]{1,0:T(8,128)(2,1)}, bf16[64,960]{1,0:T(8,128)(2,1)}, u32[]{:S(2)}, u32[]{:S(2)}) collective-permute-start(bf16[64,960]{1,0:T(8,128)(2,1)} %get-tuple-element.624), channel_id=1, source_target_pairs={{64,0},{65,1},{66,2},{67,3},{68,4},{69,5},{70,6},{71,7},{72,8},{73... | collective-permute-start | bytes 368648 | tf_op jit(solution)/shard_map/ppermute | solution.py:28
  844.8 35.9 %copy-start.6 = (bf16[1,960,320]{1,2,0:T(8,128)(2,1)S(1)}, bf16[1,960,320]{1,2,0:T(8,128)(2,1)}, u32[]{:S(2)}) copy-start(bf16[1,960,320]{1,2,0:T(8,128)(2,1)} %copy-done.4) | copy-start | bytes 1843204
  844.8 35.9 %copy-start.92 = (bf16[960]{0:T(1024)(128)(2,1)S(1)}, bf16[960]{0:T(1024)(128)(2,1)}, u32[]{:S(2)}) copy-start(bf16[960]{0:T(1024)(128)(2,1)} %copy-done.90) | copy-start | bytes 5764
  844.8 35.9 %copy-start.113 = (s32[2,64]{1,0:T(2,128)S(1)}, s32[2,64]{1,0:T(2,128)}, u32[]{:S(2)}) copy-start(s32[2,64]{1,0:T(2,128)} %param.25) | copy-start | bytes 1540
  858.6 16.9 %copy-start.52 = (bf16[2,64,320]{2,1,0:T(8,128)(2,1)S(1)}, bf16[2,64,320]{2,1,0:T(8,128)(2,1)}, u32[]{:S(2)}) copy-start(bf16[2,64,320]{2,1,0:T(8,128)(2,1)} %constant_dynamic-update-slice_fusion.1) | copy-start | bytes 245764
  1063.3 20.9 %slice-start.18 = ((s8[9830400]{0:T(1024)(128)(4,1)}), s8[1441792]{0:T(1024)(128)(4,1)S(1)}, s32[]{:S(2)}) async-start(s8[9830400]{0:T(1024)(128)(4,1)} %bitcast.935), calls=%async_computation.25 | async-start | bytes 2883584
  1132.4 373.3 %copy-start.69 = (bf16[1,2,64,960]{3,2,1,0:T(8,128)(2,1)}, bf16[1,2,64,960]{3,2,1,0:T(8,128)(2,1)S(1)}, u32[]{:S(2)}) copy-start(bf16[1,2,64,960]{3,2,1,0:T(8,128)(2,1)S(1)} %get-tuple-element.1332) | copy-start | bytes 737284
  (105 other events, 631.9 us)
Sparse Core Ops, SparseCore 0:
  11.4 71.6 all-gather.5
  86.4 66.7 all-gather.7
  156.6 81.3 all-gather.9
  241.3 82.3 all-gather.11
  326.4 69.7 all-gather.13
  1127.0 364.7 all-reduce.6
